TPU v7x, 256 devices: a whole 4x4x8 slice. The times are simulated.
256 devices in a mesh: gx: 16 (over z_hi, x, core), gy: 16 (over z_lo, y).
Axes of the slice: x: 4, y: 4, z: 8 (z_hi: 2, z_lo: 4; z = z_hi * 4 + z_lo), core: 2. Of those that a mesh axis runs over, the one named last changes fastest.
Arguments:
- intensity: float32 [32, 2048, 2048], P(None, 'gx', 'gy'), may hold values from -6 to 6
- weight: float32 [32, 2048, 2048], P(None, 'gx', 'gy'), may hold values from 0.2 to 5
- spacing: int32 [3], replicated, may hold values from 10 to 12
- anchor: int32 [3], replicated, may hold values from 0 to 5
- reach: int32 [1], replicated, may hold values from 36 to 49
Outputs:
- delta_pdf: float32 [32, 2048, 2048], P('gx', 'gy')
All inputs are finite; a program needn't handle non-finite values.
Results may differ from a plain program's by a relative error of at most 0.00007.
Values sent between devices are 32-bit elements; how exact they have to be, the bound alone decides.
A program may use at most 128 MiB of HBM per device.

v0:
```python
import functools

import jax
import jax.numpy as jnp
import ml_dtypes
import numpy as np
from jax import lax
from jax.experimental import pallas as pl
from jax.experimental.pallas import tpu as pltpu
from jax.sharding import PartitionSpec as P

MESH = pl.DeviceIdType.MESH
T = 128
EXT = T + 16


def cosine_matrix(length):
    k = np.arange(length, dtype=np.int64)
    phase = (k[:, None] * (2 * k[None, :] + 1)) % (4 * length)
    return np.cos(phase * (np.pi / (2 * length))) * np.sqrt(2.0 / length)


def split_pair(matrix):
    matrix = matrix.astype(np.float32)
    high = matrix.astype(ml_dtypes.bfloat16)
    low = (matrix - high.astype(np.float32)).astype(ml_dtypes.bfloat16)
    return high, low


def xor(a, b, bits):
    total = 0
    for i in range(bits):
        total = total + (2**i) * ((a // 2**i + b // 2**i) % 2)
    return total


def high_low(x):
    high = x.astype(jnp.bfloat16)
    return high, (x - high.astype(jnp.float32)).astype(jnp.bfloat16)


def plane_dist(position, spacing, anchor):
    offset = position - anchor
    offset = offset - spacing * jnp.floor((offset + 0.5) / spacing)
    return jnp.minimum(offset, spacing - offset)


def kernel(
    nx, ny, depth,
    i_hbm, w_hbm, sp_ref, an_ref, re_ref, chi_hbm, clo_hbm, thi_hbm, tlo_hbm,
    out_hbm,
    iv, wv, fbuf, xpack, xrecv, ypack, yrecv, flat, inside,
    recv1, fx, sbuf, recv2, acc, chi, clo, thi, tlo,
    lsem, csem, osem, hs, hr, s1, r1, s2, r2,
):
    gx = lax.axis_index("gx")
    gy = lax.axis_index("gy")
    full_x, full_y = nx * T, ny * T
    bits_x, bits_y = nx.bit_length() - 1, ny.bit_length() - 1
    left, right = (gy + ny - 1) % ny, (gy + 1) % ny
    up, down = (gx + nx - 1) % nx, (gx + 1) % nx

    loads = [
        pltpu.make_async_copy(i_hbm, iv, lsem.at[0]),
        pltpu.make_async_copy(w_hbm, wv, lsem.at[1]),
    ]
    consts = [
        pltpu.make_async_copy(src, dst, csem.at[i])
        for i, (src, dst) in enumerate(
            ((chi_hbm, chi), (clo_hbm, clo), (thi_hbm, thi), (tlo_hbm, tlo))
        )
    ]
    for cp in loads:
        cp.start()
    barrier = pltpu.get_barrier_semaphore()
    for s in range(1, nx):
        pl.semaphore_signal(barrier, inc=1, device_id=((gx + s) % nx, gy), device_id_type=MESH)
    for s in range(1, ny):
        pl.semaphore_signal(barrier, inc=1, device_id=(gx, (gy + s) % ny), device_id_type=MESH)
    for px in (up, down):
        for py in (left, right):
            pl.semaphore_signal(barrier, inc=1, device_id=(px, py), device_id_type=MESH)
    for cp in consts:
        cp.start()

    lane = lax.broadcasted_iota(jnp.int32, (EXT, T), 1)
    row = lax.broadcasted_iota(jnp.int32, (EXT, T), 0)
    xpos = gx * T - 8 + row
    in_x = (xpos >= 0) & (xpos < full_x)
    dist_x = plane_dist(
        xpos.astype(jnp.float32), sp_ref[1].astype(jnp.float32), an_ref[1].astype(jnp.float32)
    )
    for part in range(2):
        if part == 0:
            ypos = gy * T + lane
            keep = in_x
        else:
            ypos = gy * T + jnp.where(lane < T // 2, lane + T, lane - T)
            keep = in_x & (ypos >= 0) & (ypos < full_y) & ((lane < 4) | (lane >= T - 4))
        dist_y = plane_dist(
            ypos.astype(jnp.float32), sp_ref[2].astype(jnp.float32), an_ref[2].astype(jnp.float32)
        )
        hole = dist_x * dist_x + dist_y * dist_y <= re_ref[0].astype(jnp.float32)
        inside[part] = jnp.where(keep, 1.0, 0.0)
        flat[part] = jnp.where(keep & hole, 1.0, 0.0)

    for cp in loads:
        cp.wait()

    sub = lax.broadcasted_iota(jnp.int32, (8, T), 0)
    tile_lane = lax.broadcasted_iota(jnp.int32, (T, T), 1)
    ypack[...] = jnp.zeros_like(ypack)

    @pl.loop(0, depth // 4)
    def _(q):
        for arr, src in enumerate((iv, wv)):
            first = ypack[0, arr]
            second = ypack[1, arr]
            for j in range(4):
                layer = 4 * q + j
                tile = src[layer]
                mine = tile_lane // 4 == layer
                first = jnp.where(mine, pltpu.roll(tile, (4 * layer + 4) % T, 1), first)
                second = jnp.where(mine, pltpu.roll(tile, (4 * layer) % T, 1), second)
            ypack[0, arr] = first
            ypack[1, arr] = second
            for j in range(2):
                even, odd = src.at[4 * q + 2 * j], src.at[4 * q + 2 * j + 1]
                xpack[0, arr, 2 * q + j] = jnp.where(
                    sub < 4, even[0:8], pltpu.roll(odd[0:8], 4, 0)
                )
                xpack[1, arr, 2 * q + j] = jnp.where(
                    sub >= 4, even[T - 8 : T], pltpu.roll(odd[T - 8 : T], 4, 0)
                )

    pl.semaphore_wait(barrier, (nx - 1) + (ny - 1) + 4)

    halo = []
    routes = (
        (ypack.at[0], yrecv.at[0, :, pl.ds(8, T)], (gx, right)),
        (ypack.at[1], yrecv.at[1, :, pl.ds(8, T)], (gx, left)),
        (xpack.at[0], xrecv.at[1], (up, gy)),
        (xpack.at[1], xrecv.at[0], (down, gy)),
        (ypack.at[0, :, pl.ds(T - 8, 8)], yrecv.at[0, :, pl.ds(0, 8)], (down, right)),
        (ypack.at[0, :, pl.ds(0, 8)], yrecv.at[0, :, pl.ds(T + 8, 8)], (up, right)),
        (ypack.at[1, :, pl.ds(T - 8, 8)], yrecv.at[1, :, pl.ds(0, 8)], (down, left)),
        (ypack.at[1, :, pl.ds(0, 8)], yrecv.at[1, :, pl.ds(T + 8, 8)], (up, left)),
    )
    for i, (src, dst, dev) in enumerate(routes):
        cp = pltpu.make_async_remote_copy(
            src_ref=src, dst_ref=dst, send_sem=hs.at[i], recv_sem=hr.at[i],
            device_id=dev, device_id_type=MESH,
        )
        cp.start()
        halo.append(cp)
    for cp in halo:
        cp.wait()

    def blur(main, side):
        def across(a, b):
            before = pltpu.roll(jnp.where(lane == T - 1, b, a), 1, 1)
            after = pltpu.roll(jnp.where(lane == 0, b, a), T - 1, 1)
            s = (before + after) + (a + a)
            return (pltpu.roll(s, 1, 0) + pltpu.roll(s, EXT - 1, 0)) + (s + s)

        return across(main, side), across(side, main)

    def extended(arr, src, layer, half):
        top, bottom = xrecv[0, arr, layer // 2], xrecv[1, arr, layer // 2]
        if half:
            top, bottom = pltpu.roll(top, 4, 0), pltpu.roll(bottom, 4, 0)
        main = jnp.concatenate([top, src[layer], bottom], axis=0)
        before = pltpu.roll(yrecv[0, arr], (2 * T - 4 - 4 * layer) % T, 1)
        after = pltpu.roll(yrecv[1, arr], (T - 4 * layer) % T, 1)
        return main, jnp.where(lane < T // 2, after, before)

    def fill(layer, half):
        zpos = lax.broadcasted_iota(jnp.int32, (1, T), 0) + layer
        dist_z = plane_dist(
            zpos.astype(jnp.float32), sp_ref[0].astype(jnp.float32), an_ref[0].astype(jnp.float32)
        )
        zflag = jnp.where(dist_z <= 1.0, 1.0, 0.0)
        holes = [flat[part] * zflag > 0.5 for part in range(2)]
        weights = [w * inside[part] for part, w in enumerate(extended(1, wv, layer, half))]
        values = [
            jnp.where(h, 0.0, v) for h, v in zip(holes, extended(0, iv, layer, half))
        ]
        inverse = [
            1.0 / jnp.where(h, d, 1.0) for h, d in zip(holes, blur(*weights))
        ]
        for _ in range(3):
            numer = blur(*[w * v for w, v in zip(weights, values)])
            values = [
                jnp.where(h, n * r, v) for h, n, r, v in zip(holes, numer, inverse, values)
            ]
        fbuf[layer] = values[0][8 : 8 + T]

    def first_copy(layer, half, peer):
        return pltpu.make_async_remote_copy(
            src_ref=fbuf.at[layer], dst_ref=recv1.at[gx, half],
            send_sem=s1.at[layer], recv_sem=r1.at[gx, half],
            device_id=(peer, gy), device_id_type=MESH,
        )

    for half in range(2):
        @pl.loop(0, nx - 1)
        def _(t):
            peer = xor(gx, nx - 1 - t, bits_x)
            layer = 2 * peer + half
            fill(layer, half)
            first_copy(layer, half, peer).start()

    for half in range(2):
        fill(2 * gx + half, half)
        recv1[gx, half] = fbuf[2 * gx + half]

    def second_copy(half, block):
        return pltpu.make_async_remote_copy(
            src_ref=sbuf.at[half, block], dst_ref=recv2.at[gy, half],
            send_sem=s2.at[half, block], recv_sem=r2.at[gy, half],
            device_id=(gx, block), device_id_type=MESH,
        )

    groups = ny // 4
    order = [o for o in (2, 3, 1, 0) if o < groups]
    for half in range(2):
        @pl.loop(0, nx)
        def _(t):
            peer = xor(gx, t, bits_x)

            @pl.when(t > 0)
            def _():
                pltpu.make_async_remote_copy(
                    src_ref=fbuf.at[0], dst_ref=recv1.at[peer, half],
                    send_sem=s1.at[0], recv_sem=r1.at[peer, half],
                    device_id=(peer, gy), device_id_type=MESH,
                ).wait_recv()

            high, low = high_low(recv1[peer, half])
            start = pl.multiple_of(peer * T, T)
            fx[pl.ds(start, T), 0:T] = high
            fx[pl.ds(start, T), T : 2 * T] = low

        if half == 0:
            for cp in consts[:2]:
                cp.wait()
        for o in order:
            group = xor(gy // 4, o, bits_y - 2)
            start = pl.multiple_of(group * (4 * T), 4 * T)
            both = jnp.dot(
                chi[pl.ds(start, 4 * T), :], fx[...], preferred_element_type=jnp.float32
            )
            rest = jnp.dot(
                clo[pl.ds(start, 4 * T), :], fx[:, 0:T], preferred_element_type=jnp.float32
            )
            total = both[:, 0:T] + (both[:, T : 2 * T] + rest)
            for j in range(4):
                block = 4 * group + j
                sbuf[half, block] = total[j * T : (j + 1) * T]

                @pl.when(block != gy)
                def _():
                    second_copy(half, block).start()

                @pl.when(block == gy)
                def _():
                    recv2[gy, half] = sbuf[half, block]

    for cp in consts[2:]:
        cp.wait()
    outs = []
    for half in range(2):
        for o in range(groups):
            group = xor(gy // 4, o, bits_y - 2)
            parts = []
            for j in range(4):
                block = 4 * group + j

                @pl.when(block != gy)
                def _():
                    pltpu.make_async_remote_copy(
                        src_ref=sbuf.at[half, 0], dst_ref=recv2.at[block, half],
                        send_sem=s2.at[half, 0], recv_sem=r2.at[block, half],
                        device_id=(gx, block), device_id_type=MESH,
                    ).wait_recv()

                parts.append(recv2[block, half])
            high, low = high_low(jnp.concatenate(parts, axis=1))
            stacked = jnp.concatenate([high, low], axis=0)
            start = pl.multiple_of(group * (4 * T), 4 * T)

            @pl.loop(0, full_y // 512)
            def _(c):
                cols = pl.ds(pl.multiple_of(c * 512, 512), 512)
                both = jnp.dot(
                    stacked, thi[pl.ds(start, 4 * T), cols], preferred_element_type=jnp.float32
                )
                rest = jnp.dot(
                    high, tlo[pl.ds(start, 4 * T), cols], preferred_element_type=jnp.float32
                )
                total = both[0:T] + (both[T : 2 * T] + rest)
                if o == 0:
                    acc[half, :, cols] = total
                else:
                    acc[half, :, cols] += total

        cp = pltpu.make_async_copy(acc.at[half], out_hbm.at[half], osem.at[half])
        cp.start()
        outs.append(cp)

    for half in range(2):
        @pl.loop(0, nx - 1)
        def _(t):
            peer = xor(gx, nx - 1 - t, bits_x)
            first_copy(2 * peer + half, half, peer).wait_send()

        @pl.loop(1, ny)
        def _(t):
            second_copy(half, xor(gy, t, bits_y)).wait_send()
    for cp in outs:
        cp.wait()


def per_device(nx, ny, intensity, weight, spacing, anchor, reach):
    depth = intensity.shape[0]
    full_x, full_y = nx * T, ny * T
    chi, clo = split_pair(cosine_matrix(full_x))
    thi, tlo = split_pair(cosine_matrix(full_y).T)
    f32, bf16 = jnp.float32, jnp.bfloat16
    vmem, dma = pltpu.VMEM, pltpu.SemaphoreType.DMA
    anywhere = pl.BlockSpec(memory_space=pl.ANY)
    scalars = pl.BlockSpec(memory_space=pltpu.SMEM)
    return pl.pallas_call(
        functools.partial(kernel, nx, ny, depth),
        out_shape=jax.ShapeDtypeStruct((2, T, full_y), f32),
        in_specs=[anywhere] * 2 + [scalars] * 3 + [anywhere] * 4,
        out_specs=anywhere,
        scratch_shapes=[
            vmem((depth, T, T), f32),
            vmem((depth, T, T), f32),
            vmem((depth, T, T), f32),
            vmem((2, 2, depth // 2, 8, T), f32),
            vmem((2, 2, depth // 2, 8, T), f32),
            vmem((2, 2, T, T), f32),
            vmem((2, 2, EXT, T), f32),
            vmem((2, EXT, T), f32),
            vmem((2, EXT, T), f32),
            vmem((nx, 2, T, T), f32),
            vmem((full_x, 2 * T), bf16),
            vmem((2, ny, T, T), f32),
            vmem((ny, 2, T, T), f32),
            vmem((2, T, full_y), f32),
            vmem((full_x, full_x), bf16),
            vmem((full_x, full_x), bf16),
            vmem((full_y, full_y), bf16),
            vmem((full_y, full_y), bf16),
            dma((2,)), dma((4,)), dma((2,)), dma((8,)), dma((8,)),
            dma((depth,)), dma((nx, 2)), dma((2, ny)), dma((ny, 2)),
        ],
        compiler_params=pltpu.CompilerParams(
            collective_id=0, has_side_effects=True, vmem_limit_bytes=60 * 2**20
        ),
    )(intensity, weight, spacing, anchor, reach, chi, clo, thi, tlo)


def solution(mesh):
    nx, ny = mesh.shape["gx"], mesh.shape["gy"]
    in_specs = (P(None, "gx", "gy"), P(None, "gx", "gy"), P(), P(), P())
    return jax.shard_map(
        functools.partial(per_device, nx, ny),
        mesh=mesh, in_specs=in_specs, out_specs=P("gx", "gy", None), check_vma=False,
    )
```

profile of v0, /device:TPU:57, one launch (start us, length us, event | category | flops | bytes accessed | tf_op | source)
XLA Modules:
  0.0 123.2 jit_solution(14634191069486594121)
XLA Ops:
  0.7 119.4 %shard_map.91 = f32[2,128,2048]{2,1,0:T(8,128)} custom-call(f32[32,128,128]{2,1,0:T(8,128)} %i_hbm.1, f32[32,128,128]{2,1,0:T(8,128)} %w_hbm.1, s32[3]{0:T(128)} %sp_ref.1, s32[3]{0:T(128)} %an_ref.1, s32[1]{0:T(128)S(6)} %copy.11.re_ref, bf16[2048,2048]{1,0:T(8,128)(2,1)} %constant.8.clone.chi_hbm, bf16[2048,2048]{1,0:T(8,128)(2,1)} %constant.9.clone.clo_hbm, ...), custom_call_target="tpu_custom_call" | custom-call | tf_op jit(solution)/shard_map/pallas_call | solution.py:333
  120.0 3.1 %copy.12 = f32[2,128,2048]{2,1,0:T(8,128)} copy(f32[2,128,2048]{2,1,0:T(8,128)} %shard_map.91) | data formatting | bytes 4194304
where the time goes:
time: 123 us
  Pallas kernels  119 us (97%)
  local copies, waits for them, and re-layouts  3.14 us (3%)
    pallas_call x1, Pallas kernels, per_device(): pl.pallas_call(functools.partial(kernel, nx, ny, depth), out_shape=jax.Sh...  119 us
    unnamed x1, local copies, waits for them, and re-layouts  3.14 us

commit v1 on v0

--- a/solution.py
+++ b/solution.py
@@ -45,10 +45,14 @@
     return jnp.minimum(offset, spacing - offset)
 
 
+def hole_slots(depth):
+    return 3 * (depth // 10 + 1) + 3 * (depth // 10 + 1) % 2
+
+
 def kernel(
     nx, ny, depth,
     i_hbm, w_hbm, sp_ref, an_ref, re_ref, chi_hbm, clo_hbm, thi_hbm, tlo_hbm,
-    out_hbm,
+    out0_hbm, out1_hbm,
     iv, wv, fbuf, xpack, xrecv, ypack, yrecv, flat, inside,
     recv1, fx, sbuf, recv2, acc, chi, clo, thi, tlo,
     lsem, csem, osem, hs, hr, s1, r1, s2, r2,
@@ -56,6 +60,7 @@
     gx = lax.axis_index("gx")
     gy = lax.axis_index("gy")
     full_x, full_y = nx * T, ny * T
+    slots = hole_slots(depth)
     bits_x, bits_y = nx.bit_length() - 1, ny.bit_length() - 1
     left, right = (gy + ny - 1) % ny, (gy + 1) % ny
     up, down = (gx + nx - 1) % nx, (gx + 1) % nx
@@ -108,53 +113,50 @@
         cp.wait()
 
     sub = lax.broadcasted_iota(jnp.int32, (8, T), 0)
-    tile_lane = lax.broadcasted_iota(jnp.int32, (T, T), 1)
-    ypack[...] = jnp.zeros_like(ypack)
-
-    @pl.loop(0, depth // 4)
-    def _(q):
-        for arr, src in enumerate((iv, wv)):
-            first = ypack[0, arr]
-            second = ypack[1, arr]
-            for j in range(4):
-                layer = 4 * q + j
-                tile = src[layer]
-                mine = tile_lane // 4 == layer
-                first = jnp.where(mine, pltpu.roll(tile, (4 * layer + 4) % T, 1), first)
-                second = jnp.where(mine, pltpu.roll(tile, (4 * layer) % T, 1), second)
-            ypack[0, arr] = first
-            ypack[1, arr] = second
-            for j in range(2):
-                even, odd = src.at[4 * q + 2 * j], src.at[4 * q + 2 * j + 1]
-                xpack[0, arr, 2 * q + j] = jnp.where(
-                    sub < 4, even[0:8], pltpu.roll(odd[0:8], 4, 0)
-                )
-                xpack[1, arr, 2 * q + j] = jnp.where(
-                    sub >= 4, even[T - 8 : T], pltpu.roll(odd[T - 8 : T], 4, 0)
-                )
+    group = lax.broadcasted_iota(jnp.int32, (T, T), 1) // 4
+    first = second = jnp.zeros((T, T), jnp.float32)
+    for arr, src in enumerate((iv, wv)):
+        ends = []
+        for slot in range(slots):
+            layer = an_ref[0] + (slot // 3) * sp_ref[0] + (slot % 3 - 1)
+            tile = src[jnp.clip(layer, 0, depth - 1)]
+            place = slot + arr * slots
+            first = jnp.where(group == place, pltpu.roll(tile, (4 * place + 4) % T, 1), first)
+            second = jnp.where(group == place, pltpu.roll(tile, (4 * place) % T, 1), second)
+            ends.append((tile[0:8], tile[T - 8 : T]))
+        for pair in range(slots // 2):
+            even, odd = ends[2 * pair], ends[2 * pair + 1]
+            xpack[0, arr, pair] = jnp.where(sub < 4, even[0], pltpu.roll(odd[0], 4, 0))
+            xpack[1, arr, pair] = jnp.where(sub >= 4, even[1], pltpu.roll(odd[1], 4, 0))
+    ypack[0] = first
+    ypack[1] = second
 
     pl.semaphore_wait(barrier, (nx - 1) + (ny - 1) + 4)
 
+    has_up, has_down = gx > 0, gx < nx - 1
+    has_left, has_right = gy > 0, gy < ny - 1
+    ends, starts, rows = pl.ds(T - 8, 8), pl.ds(0, 8), pl.ds(8, T)
+    before, after = pl.ds(0, 8), pl.ds(T + 8, 8)
+    routes = (
+        (ypack.at[0], yrecv.at[0, rows], (gx, right), has_right, has_left),
+        (ypack.at[1], yrecv.at[1, rows], (gx, left), has_left, has_right),
+        (xpack.at[0], xrecv.at[1], (up, gy), has_up, has_down),
+        (xpack.at[1], xrecv.at[0], (down, gy), has_down, has_up),
+        (ypack.at[0, ends], yrecv.at[0, before], (down, right), has_down & has_right, has_up & has_left),
+        (ypack.at[0, starts], yrecv.at[0, after], (up, right), has_up & has_right, has_down & has_left),
+        (ypack.at[1, ends], yrecv.at[1, before], (down, left), has_down & has_left, has_up & has_right),
+        (ypack.at[1, starts], yrecv.at[1, after], (up, left), has_up & has_left, has_down & has_right),
+    )
     halo = []
-    routes = (
-        (ypack.at[0], yrecv.at[0, :, pl.ds(8, T)], (gx, right)),
-        (ypack.at[1], yrecv.at[1, :, pl.ds(8, T)], (gx, left)),
-        (xpack.at[0], xrecv.at[1], (up, gy)),
-        (xpack.at[1], xrecv.at[0], (down, gy)),
-        (ypack.at[0, :, pl.ds(T - 8, 8)], yrecv.at[0, :, pl.ds(0, 8)], (down, right)),
-        (ypack.at[0, :, pl.ds(0, 8)], yrecv.at[0, :, pl.ds(T + 8, 8)], (up, right)),
-        (ypack.at[1, :, pl.ds(T - 8, 8)], yrecv.at[1, :, pl.ds(0, 8)], (down, left)),
-        (ypack.at[1, :, pl.ds(0, 8)], yrecv.at[1, :, pl.ds(T + 8, 8)], (up, left)),
-    )
-    for i, (src, dst, dev) in enumerate(routes):
+    for i, (src, dst, dev, sends, receives) in enumerate(routes):
         cp = pltpu.make_async_remote_copy(
             src_ref=src, dst_ref=dst, send_sem=hs.at[i], recv_sem=hr.at[i],
             device_id=dev, device_id_type=MESH,
         )
-        cp.start()
-        halo.append(cp)
-    for cp in halo:
-        cp.wait()
+        halo.append((cp, sends, receives))
+        pl.when(sends)(cp.start)
+    for cp, _, receives in halo:
+        pl.when(receives)(cp.wait_recv)
 
     def blur(main, side):
         def across(a, b):
@@ -165,25 +167,37 @@
 
         return across(main, side), across(side, main)
 
-    def extended(arr, src, layer, half):
-        top, bottom = xrecv[0, arr, layer // 2], xrecv[1, arr, layer // 2]
-        if half:
-            top, bottom = pltpu.roll(top, 4, 0), pltpu.roll(bottom, 4, 0)
+    def extended(arr, src, layer, slot):
+        top, bottom = xrecv[0, arr, slot // 2], xrecv[1, arr, slot // 2]
+        odd = jnp.full((8, T), slot % 2, jnp.int32) == 1
+        top = jnp.where(odd, pltpu.roll(top, 4, 0), top)
+        bottom = jnp.where(odd, pltpu.roll(bottom, 4, 0), bottom)
         main = jnp.concatenate([top, src[layer], bottom], axis=0)
-        before = pltpu.roll(yrecv[0, arr], (2 * T - 4 - 4 * layer) % T, 1)
-        after = pltpu.roll(yrecv[1, arr], (T - 4 * layer) % T, 1)
+        shift = 2 * T - 4 * (slot + arr * slots)
+        before = pltpu.roll(yrecv[0], (shift - 4) % T, 1)
+        after = pltpu.roll(yrecv[1], shift % T, 1)
         return main, jnp.where(lane < T // 2, after, before)
 
-    def fill(layer, half):
+    def fill(layer):
+        place = layer - an_ref[0] + 1
+        turn = 0
+        for m in range(1, slots // 3):
+            turn = turn + (place >= m * sp_ref[0]).astype(jnp.int32)
+        slot = 3 * turn + jnp.clip(place - turn * sp_ref[0], 0, 2)
         zpos = lax.broadcasted_iota(jnp.int32, (1, T), 0) + layer
         dist_z = plane_dist(
             zpos.astype(jnp.float32), sp_ref[0].astype(jnp.float32), an_ref[0].astype(jnp.float32)
         )
         zflag = jnp.where(dist_z <= 1.0, 1.0, 0.0)
-        holes = [flat[part] * zflag > 0.5 for part in range(2)]
-        weights = [w * inside[part] for part, w in enumerate(extended(1, wv, layer, half))]
+        masks = [flat[part] * zflag for part in range(2)]
+        holes = [m > 0.5 for m in masks]
+        weights = [
+            jnp.where(inside[part] > 0.5, w, 0.0)
+            for part, w in enumerate(extended(1, wv, layer, slot))
+        ]
         values = [
-            jnp.where(h, 0.0, v) for h, v in zip(holes, extended(0, iv, layer, half))
+            jnp.where(inside[part] - masks[part] > 0.5, v, 0.0)
+            for part, v in enumerate(extended(0, iv, layer, slot))
         ]
         inverse = [
             1.0 / jnp.where(h, d, 1.0) for h, d in zip(holes, blur(*weights))
@@ -207,11 +221,11 @@
         def _(t):
             peer = xor(gx, nx - 1 - t, bits_x)
             layer = 2 * peer + half
-            fill(layer, half)
+            fill(layer)
             first_copy(layer, half, peer).start()
 
     for half in range(2):
-        fill(2 * gx + half, half)
+        fill(2 * gx + half)
         recv1[gx, half] = fbuf[2 * gx + half]
 
     def second_copy(half, block):
@@ -255,8 +269,9 @@
             )
             total = both[:, 0:T] + (both[:, T : 2 * T] + rest)
             for j in range(4):
-                block = 4 * group + j
-                sbuf[half, block] = total[j * T : (j + 1) * T]
+                sbuf[half, 4 * group + j] = total[j * T : (j + 1) * T]
+            for j in range(4):
+                block = 4 * group + xor(gy % 4, j, 2)
 
                 @pl.when(block != gy)
                 def _():
@@ -304,7 +319,9 @@
                 else:
                     acc[half, :, cols] += total
 
-        cp = pltpu.make_async_copy(acc.at[half], out_hbm.at[half], osem.at[half])
+        cp = pltpu.make_async_copy(
+            acc.at[half], (out0_hbm, out1_hbm)[half].at[0], osem.at[half]
+        )
         cp.start()
         outs.append(cp)
 
@@ -317,6 +334,8 @@
         @pl.loop(1, ny)
         def _(t):
             second_copy(half, xor(gy, t, bits_y)).wait_send()
+    for cp, sends, _ in halo:
+        pl.when(sends)(cp.wait_send)
     for cp in outs:
         cp.wait()
 
@@ -330,19 +349,20 @@
     vmem, dma = pltpu.VMEM, pltpu.SemaphoreType.DMA
     anywhere = pl.BlockSpec(memory_space=pl.ANY)
     scalars = pl.BlockSpec(memory_space=pltpu.SMEM)
-    return pl.pallas_call(
+    slots = hole_slots(depth)
+    first, second = pl.pallas_call(
         functools.partial(kernel, nx, ny, depth),
-        out_shape=jax.ShapeDtypeStruct((2, T, full_y), f32),
+        out_shape=[jax.ShapeDtypeStruct((1, T, full_y), f32)] * 2,
         in_specs=[anywhere] * 2 + [scalars] * 3 + [anywhere] * 4,
-        out_specs=anywhere,
+        out_specs=[anywhere] * 2,
         scratch_shapes=[
             vmem((depth, T, T), f32),
             vmem((depth, T, T), f32),
             vmem((depth, T, T), f32),
-            vmem((2, 2, depth // 2, 8, T), f32),
-            vmem((2, 2, depth // 2, 8, T), f32),
-            vmem((2, 2, T, T), f32),
-            vmem((2, 2, EXT, T), f32),
+            vmem((2, 2, slots // 2, 8, T), f32),
+            vmem((2, 2, slots // 2, 8, T), f32),
+            vmem((2, T, T), f32),
+            vmem((2, EXT, T), f32),
             vmem((2, EXT, T), f32),
             vmem((2, EXT, T), f32),
             vmem((nx, 2, T, T), f32),
@@ -361,6 +381,7 @@
             collective_id=0, has_side_effects=True, vmem_limit_bytes=60 * 2**20
         ),
     )(intensity, weight, spacing, anchor, reach, chi, clo, thi, tlo)
+    return jnp.concatenate([first, second], axis=0)
 
 
 def solution(mesh):

time: 123 us -> 121 us (0.984)
  local copies, waits for them, and re-layouts: 3.14 us -> 0 us
  other arithmetic: 0 us -> 3.09 us
  Pallas kernels: 119 us -> 116 us
    unnamed x1 -> x0, local copies, waits for them, and re-layouts: 3.14 us -> none
    concatenate x0 -> x1, other arithmetic: none -> 3.09 us  [per_device(): return jnp.concatenate([first, second], axis=0)]
    pallas_call x1, Pallas kernels: 119 us -> 116 us  [per_device(): pl.pallas_call(functools.partial(kernel, nx, ny, depth), out_shape=[jax.S...]
where the time goes in v1:
time: 121 us; the launch traced here: 120 us
  Pallas kernels  116 us (96%)
  other arithmetic  3.09 us (3%)
    pallas_call x1, Pallas kernels, per_device(): pl.pallas_call(functools.partial(kernel, nx, ny, depth), out_shape=[jax.S...  116 us
    concatenate x1, other arithmetic, per_device(): return jnp.concatenate([first, second], axis=0)  3.09 us

profile of v1, /device:TPU:57, one launch (start us, length us, event | category | flops | bytes accessed | tf_op | source)
XLA Modules:
  0.0 120.2 jit_solution(10872045007610283954)
XLA Ops:
  0.7 116.5 %shard_map.91 = (f32[1,128,2048]{2,1,0:T(8,128)}, f32[1,128,2048]{2,1,0:T(8,128)}) custom-call(f32[32,128,128]{2,1,0:T(8,128)} %i_hbm.1, f32[32,128,128]{2,1,0:T(8,128)} %w_hbm.1, s32[3]{0:T(128)} %sp_ref.1, s32[3]{0:T(128)} %an_ref.1, s32[1]{0:T(128)S(6)} %copy.10.re_ref, bf16[2048,2048]{1,0:T(8,128)(2,1)} %constant.8.clone.chi_hbm, ...), custom_call_target="tpu_custom_call" | custom-call | tf_op jit(solution)/shard_map/pallas_call | solution.py:353
  117.1 3.1 %pad_maximum_fusion = f32[2,128,2048]{2,1,0:T(8,128)} fusion(f32[1,128,2048]{2,1,0:T(8,128)} %get-tuple-element.8, f32[1,128,2048]{2,1,0:T(8,128)} %get-tuple-element.7), kind=kLoop, calls=%fused_computation | loop fusion | flops 524288 | bytes 4194304 | tf_op jit(solution)/shard_map/concatenate | solution.py:384

commit v2 on v1

--- a/solution.py
+++ b/solution.py
@@ -52,10 +52,10 @@
 def kernel(
     nx, ny, depth,
     i_hbm, w_hbm, sp_ref, an_ref, re_ref, chi_hbm, clo_hbm, thi_hbm, tlo_hbm,
-    out0_hbm, out1_hbm,
+    acc,
     iv, wv, fbuf, xpack, xrecv, ypack, yrecv, flat, inside,
-    recv1, fx, sbuf, recv2, acc, chi, clo, thi, tlo,
-    lsem, csem, osem, hs, hr, s1, r1, s2, r2,
+    recv1, fx, sbuf, recv2, chi, clo, thi, tlo,
+    lsem, csem, hs, hr, s1, r1, s2, r2,
 ):
     gx = lax.axis_index("gx")
     gy = lax.axis_index("gy")
@@ -85,8 +85,6 @@
     for px in (up, down):
         for py in (left, right):
             pl.semaphore_signal(barrier, inc=1, device_id=(px, py), device_id_type=MESH)
-    for cp in consts:
-        cp.start()
 
     lane = lax.broadcasted_iota(jnp.int32, (EXT, T), 1)
     row = lax.broadcasted_iota(jnp.int32, (EXT, T), 0)
@@ -109,13 +107,11 @@
         inside[part] = jnp.where(keep, 1.0, 0.0)
         flat[part] = jnp.where(keep & hole, 1.0, 0.0)
 
-    for cp in loads:
-        cp.wait()
-
     sub = lax.broadcasted_iota(jnp.int32, (8, T), 0)
     group = lax.broadcasted_iota(jnp.int32, (T, T), 1) // 4
     first = second = jnp.zeros((T, T), jnp.float32)
     for arr, src in enumerate((iv, wv)):
+        loads[arr].wait()
         ends = []
         for slot in range(slots):
             layer = an_ref[0] + (slot // 3) * sp_ref[0] + (slot % 3 - 1)
@@ -155,6 +151,8 @@
         )
         halo.append((cp, sends, receives))
         pl.when(sends)(cp.start)
+    for cp in consts:
+        cp.start()
     for cp, _, receives in halo:
         pl.when(receives)(cp.wait_recv)
 
@@ -283,7 +281,6 @@
 
     for cp in consts[2:]:
         cp.wait()
-    outs = []
     for half in range(2):
         for o in range(groups):
             group = xor(gy // 4, o, bits_y - 2)
@@ -319,11 +316,6 @@
                 else:
                     acc[half, :, cols] += total
 
-        cp = pltpu.make_async_copy(
-            acc.at[half], (out0_hbm, out1_hbm)[half].at[0], osem.at[half]
-        )
-        cp.start()
-        outs.append(cp)
 
     for half in range(2):
         @pl.loop(0, nx - 1)
@@ -336,8 +328,6 @@
             second_copy(half, xor(gy, t, bits_y)).wait_send()
     for cp, sends, _ in halo:
         pl.when(sends)(cp.wait_send)
-    for cp in outs:
-        cp.wait()
 
 
 def per_device(nx, ny, intensity, weight, spacing, anchor, reach):
@@ -350,11 +340,11 @@
     anywhere = pl.BlockSpec(memory_space=pl.ANY)
     scalars = pl.BlockSpec(memory_space=pltpu.SMEM)
     slots = hole_slots(depth)
-    first, second = pl.pallas_call(
+    return pl.pallas_call(
         functools.partial(kernel, nx, ny, depth),
-        out_shape=[jax.ShapeDtypeStruct((1, T, full_y), f32)] * 2,
+        out_shape=pltpu.VMEM((2, T, full_y), f32),
         in_specs=[anywhere] * 2 + [scalars] * 3 + [anywhere] * 4,
-        out_specs=[anywhere] * 2,
+        out_specs=pl.BlockSpec(memory_space=pltpu.VMEM),
         scratch_shapes=[
             vmem((depth, T, T), f32),
             vmem((depth, T, T), f32),
@@ -369,19 +359,17 @@
             vmem((full_x, 2 * T), bf16),
             vmem((2, ny, T, T), f32),
             vmem((ny, 2, T, T), f32),
-            vmem((2, T, full_y), f32),
             vmem((full_x, full_x), bf16),
             vmem((full_x, full_x), bf16),
             vmem((full_y, full_y), bf16),
             vmem((full_y, full_y), bf16),
-            dma((2,)), dma((4,)), dma((2,)), dma((8,)), dma((8,)),
+            dma((2,)), dma((4,)), dma((8,)), dma((8,)),
             dma((depth,)), dma((nx, 2)), dma((2, ny)), dma((ny, 2)),
         ],
         compiler_params=pltpu.CompilerParams(
-            collective_id=0, has_side_effects=True, vmem_limit_bytes=60 * 2**20
+            collective_id=0, has_side_effects=True, vmem_limit_bytes=54 * 2**20
         ),
     )(intensity, weight, spacing, anchor, reach, chi, clo, thi, tlo)
-    return jnp.concatenate([first, second], axis=0)
 
 
 def solution(mesh):

time: 121 us -> 119 us (0.983)
  other arithmetic: 3.09 us -> 0 us
  local copies, waits for them, and re-layouts: 0 us -> 1.32 us
    concatenate x1 -> x0, other arithmetic: 3.09 us -> none  [per_device(): return jnp.concatenate([first, second], axis=0)]
    unnamed x0 -> x1, local copies, waits for them, and re-layouts: none -> 1.32 us
where the time goes in v2:
time: 119 us; the launch traced here: 118 us
  Pallas kernels  116 us (97%)
  local copies, waits for them, and re-layouts  1.32 us (1%)
    pallas_call x1, Pallas kernels, per_device(): pl.pallas_call(functools.partial(kernel, nx, ny, depth), out_shape=pltpu....  116 us

profile of v2, /device:TPU:57, one launch (start us, length us, event | category | flops | bytes accessed | tf_op | source)
XLA Modules:
  0.0 118.4 jit_solution(13384968344334650465)
XLA Ops:
  0.7 116.4 %shard_map.91 = f32[2,128,2048]{2,1,0:T(8,128)S(1)} custom-call(f32[32,128,128]{2,1,0:T(8,128)} %i_hbm.1, f32[32,128,128]{2,1,0:T(8,128)} %w_hbm.1, s32[3]{0:T(128)} %sp_ref.1, s32[3]{0:T(128)} %an_ref.1, s32[1]{0:T(128)S(6)} %copy.12.re_ref, bf16[2048,2048]{1,0:T(8,128)(2,1)} %constant.8.clone.chi_hbm, bf16[2048,2048]{1,0:T(8,128)(2,1)} %constant.9.clone.clo_hbm, ...), custom_call_target="tpu_custom_call" | custom-call | tf_op jit(solution)/shard_map/pallas_call | solution.py:343
  117.1 1.3 %copy.11 = f32[2,128,2048]{2,1,0:T(8,128)} copy(f32[2,128,2048]{2,1,0:T(8,128)S(1)} %shard_map.91) | data formatting | bytes 4194304

commit v3 on v2

--- a/solution.py
+++ b/solution.py
@@ -220,11 +220,15 @@
             peer = xor(gx, nx - 1 - t, bits_x)
             layer = 2 * peer + half
             fill(layer)
+
+            if half == 1:
+                first_copy(layer - 1, 0, peer).wait_send()
             first_copy(layer, half, peer).start()
 
-    for half in range(2):
-        fill(2 * gx + half)
-        recv1[gx, half] = fbuf[2 * gx + half]
+        if half == 0:
+            for own in range(2):
+                fill(2 * gx + own)
+                recv1[gx, own] = fbuf[2 * gx + own]
 
     def second_copy(half, block):
         return pltpu.make_async_remote_copy(
@@ -233,7 +237,20 @@
             device_id=(gx, block), device_id_type=MESH,
         )
 
+    def start_group(half, group):
+        for j in range(4):
+            block = 4 * group + xor(gy % 4, j, 2)
+
+            @pl.when(block != gy)
+            def _():
+                second_copy(half, block).start()
+
+            @pl.when(block == gy)
+            def _():
+                recv2[gy, half] = sbuf[half, gy]
+
     groups = ny // 4
+    late = min(3, groups - 1)
     order = [o for o in (2, 3, 1, 0) if o < groups]
     for half in range(2):
         @pl.loop(0, nx)
@@ -247,6 +264,11 @@
                     send_sem=s1.at[0], recv_sem=r1.at[peer, half],
                     device_id=(peer, gy), device_id_type=MESH,
                 ).wait_recv()
+
+            if half == 1:
+                @pl.when(t == nx - 2)
+                def _():
+                    start_group(0, xor(gy // 4, late, bits_y - 2))
 
             high, low = high_low(recv1[peer, half])
             start = pl.multiple_of(peer * T, T)
@@ -268,25 +290,22 @@
             total = both[:, 0:T] + (both[:, T : 2 * T] + rest)
             for j in range(4):
                 sbuf[half, 4 * group + j] = total[j * T : (j + 1) * T]
-            for j in range(4):
-                block = 4 * group + xor(gy % 4, j, 2)
-
-                @pl.when(block != gy)
-                def _():
-                    second_copy(half, block).start()
-
-                @pl.when(block == gy)
-                def _():
-                    recv2[gy, half] = sbuf[half, block]
+            if half == 1 or o != late:
+                start_group(half, group)
 
     for cp in consts[2:]:
         cp.wait()
     for half in range(2):
-        for o in range(groups):
-            group = xor(gy // 4, o, bits_y - 2)
+        steps = [(o, 0, 4) for o in range(groups)]
+        if half == 1:
+            steps[-1:] = [(groups - 1, 0, 2), (groups - 1, 1, 2)]
+        for o, part, count in steps:
+            first = 4 * xor(gy // 4, o, bits_y - 2)
+            if count == 2:
+                first = first + 2 * xor(gy % 4 // 2, part, 1)
             parts = []
-            for j in range(4):
-                block = 4 * group + j
+            for j in range(count):
+                block = first + j
 
                 @pl.when(block != gy)
                 def _():
@@ -299,29 +318,30 @@
                 parts.append(recv2[block, half])
             high, low = high_low(jnp.concatenate(parts, axis=1))
             stacked = jnp.concatenate([high, low], axis=0)
-            start = pl.multiple_of(group * (4 * T), 4 * T)
+            rows = pl.ds(pl.multiple_of(first * T, count * T), count * T)
 
             @pl.loop(0, full_y // 512)
             def _(c):
                 cols = pl.ds(pl.multiple_of(c * 512, 512), 512)
                 both = jnp.dot(
-                    stacked, thi[pl.ds(start, 4 * T), cols], preferred_element_type=jnp.float32
+                    stacked, thi[rows, cols], preferred_element_type=jnp.float32
                 )
                 rest = jnp.dot(
-                    high, tlo[pl.ds(start, 4 * T), cols], preferred_element_type=jnp.float32
+                    high, tlo[rows, cols], preferred_element_type=jnp.float32
                 )
                 total = both[0:T] + (both[T : 2 * T] + rest)
-                if o == 0:
+                if o == 0 and part == 0:
                     acc[half, :, cols] = total
                 else:
                     acc[half, :, cols] += total
 
 
     for half in range(2):
-        @pl.loop(0, nx - 1)
-        def _(t):
-            peer = xor(gx, nx - 1 - t, bits_x)
-            first_copy(2 * peer + half, half, peer).wait_send()
+        if half == 1:
+            @pl.loop(0, nx - 1)
+            def _(t):
+                peer = xor(gx, nx - 1 - t, bits_x)
+                first_copy(2 * peer + half, half, peer).wait_send()
 
         @pl.loop(1, ny)
         def _(t):

time: 119 us -> 118 us (level); the launches traced: 118 us -> 116 us
  Pallas kernels: 116 us -> 114 us
    pallas_call x1, Pallas kernels: 116 us -> 114 us  [per_device(): pl.pallas_call(functools.partial(kernel, nx, ny, depth), out_shape=pltpu....]
where the time goes in v3:
time: 118 us; the launch traced here: 116 us
  Pallas kernels  114 us (97%)
  local copies, waits for them, and re-layouts  1.32 us (1%)
    pallas_call x1, Pallas kernels, per_device(): pl.pallas_call(functools.partial(kernel, nx, ny, depth), out_shape=pltpu....  114 us

profile of v3, /device:TPU:57, one launch (start us, length us, event | category | flops | bytes accessed | tf_op | source)
XLA Modules:
  0.0 116.2 jit_solution(5046391071813063930)
XLA Ops:
  0.7 114.2 %shard_map.91 = f32[2,128,2048]{2,1,0:T(8,128)S(1)} custom-call(f32[32,128,128]{2,1,0:T(8,128)} %i_hbm.1, f32[32,128,128]{2,1,0:T(8,128)} %w_hbm.1, s32[3]{0:T(128)} %sp_ref.1, s32[3]{0:T(128)} %an_ref.1, s32[1]{0:T(128)S(6)} %copy.12.re_ref, bf16[2048,2048]{1,0:T(8,128)(2,1)} %constant.8.clone.chi_hbm, bf16[2048,2048]{1,0:T(8,128)(2,1)} %constant.9.clone.clo_hbm, ...), custom_call_target="tpu_custom_call" | custom-call | tf_op jit(solution)/shard_map/pallas_call | solution.py:363
  114.9 1.3 %copy.11 = f32[2,128,2048]{2,1,0:T(8,128)} copy(f32[2,128,2048]{2,1,0:T(8,128)S(1)} %shard_map.91) | data formatting | bytes 4194304
